TPU v7x, 32 devices: a whole 2x2x4 slice. The times are simulated.
32 devices in a mesh: gx: 4 (over x, core), gy: 8 (over z, y).
Axes of the slice: x: 2, y: 2, z: 4, core: 2. Of those that a mesh axis runs over, the one named last changes fastest.
Arguments:
- state_field: float32 [128, 128, 16, 256], P('gx', 'gy'), may hold values from -80 to 80
- start_basis: float32 [256, 32], replicated, may hold values from -6 to 6
Outputs:
- core_tensor: float32 [128, 128, 512], P('gx', 'gy')
- z_factor: float32 [256, 32], replicated
- x_triangle: float32 [128, 128], replicated
All inputs are finite; a program needn't handle non-finite values.
Results may differ from a plain program's by a relative error of at most 0.0003.
Values sent between devices are 32-bit elements; how exact they have to be, the bound alone decides.
No kernel may reach another device: no remote copies, remote signals or barrier semaphores. Data moves between devices by JAX's collectives and lax.ppermute only.
A program may use at most 64 MiB of HBM per device.

v0:
```python
import jax
import jax.numpy as jnp
from jax import lax
from jax.sharding import PartitionSpec as P

ITERS = 3
precise = lax.Precision.HIGHEST


def orthonormal(image):
    for repeat in range(2):
        inner_gram = jnp.dot(image.T, image, precision=precise, preferred_element_type=jnp.float32)
        lower_factor = jnp.linalg.cholesky(inner_gram)
        image = lax.linalg.triangular_solve(
            lower_factor, image, left_side=False, lower=True, transpose_a=True
        )
    return image


def local(state_field, start_basis):
    x_cells, y_cells, species, z_cells = state_field.shape
    unfolded = state_field.reshape(x_cells * y_cells * species, z_cells)
    local_gram = lax.dot_general(
        unfolded,
        unfolded,
        (((0,), (0,)), ((), ())),
        precision=precise,
        preferred_element_type=jnp.float32,
    )
    z_basis = start_basis
    gram_z = lax.psum(local_gram, ("gx", "gy"))
    for iteration in range(ITERS):
        z_basis = orthonormal(
            jnp.dot(gram_z, z_basis, precision=precise, preferred_element_type=jnp.float32)
        )
    rank_kept = z_basis.shape[1]
    core_rows = jnp.dot(unfolded, z_basis, precision=precise, preferred_element_type=jnp.float32)
    core_tensor = core_rows.reshape(x_cells, y_cells, species * rank_kept)
    own_rows = core_tensor.reshape(x_cells, -1)
    row_piece = lax.all_gather(core_tensor, "gx", axis=0, tiled=True)
    piece_rows = row_piece.reshape(row_piece.shape[0], -1)
    product = jnp.dot(own_rows, piece_rows.T, precision=precise, preferred_element_type=jnp.float32)
    summed_row = lax.psum(product, "gy")
    gram_x = lax.all_gather(summed_row, "gx", axis=0, tiled=True)
    column_count = y_cells * lax.axis_size("gy") * species * rank_kept
    x_triangle = jnp.linalg.cholesky(gram_x).T / jnp.sqrt(jnp.float32(column_count))
    return (core_tensor, z_basis, x_triangle)


def solution(mesh):
    return jax.shard_map(
        local,
        mesh=mesh,
        in_specs=(P("gx", "gy", None, None), P()),
        out_specs=(P("gx", "gy", None), P(), P()),
        check_vma=False,
    )
```

profile of v0, /device:TPU:0, one launch (start us, length us, event | category | flops | bytes accessed | tf_op | source)
XLA Modules:
  0.0 325.5 jit_solution(4373195180380664984)
XLA Ops:
  7.2 17.8 %convolution_bitcast_fusion.1 = f32[256,256]{1,0:T(8,128)} fusion(f32[32,16,16,256]{3,2,1,0:T(8,128)} %param.5), kind=kOutput, calls=%fused_computation.1 | convolution fusion | flops 6442450944 | bytes 8650752 | tf_op jit(solution)/shard_map/dot_general | solution.py:23
  25.3 129.2 %all-reduce.2.cloned.1.call-done = f32[256,256]{1,0:T(8,128)} async-done(((f32[256,256]{1,0:T(8,128)}), f32[256,256]{1,0:T(8,128)}) %all-reduce.2.cloned.1.call-update) | async-done | bytes 262160 | tf_op jit(solution)/shard_map/psum | solution.py:31
  154.5 1.3 fusion.29
  156.1 2.9 cholesky.142
  159.7 0.7 fusion.1
  160.3 2.4 custom-call.13
  163.2 2.9 cholesky.153
  166.8 0.7 fusion.2
  167.5 2.4 custom-call.14
  170.2 1.3 fusion.32
  171.7 2.9 cholesky.164
  175.3 0.7 fusion.3
  176.0 2.4 custom-call.15
  178.9 2.9 cholesky.175
  183.2 2.4 custom-call.16
  185.9 1.3 fusion.35
  187.4 2.9 cholesky.186
  191.7 2.4 custom-call.17
  194.6 2.9 cholesky.197
  198.9 2.4 custom-call.18
  201.6 10.1 %convolution_bitcast_fusion = f32[8192,32]{0,1:T(8,128)S(1)} fusion(f32[256,32]{0,1:T(8,128)S(1)} %convolution_bitcast_fusion.2, f32[8192,256]{1,0:T(8,128)} %bitcast.112), kind=kOutput, calls=%fused_computation | convolution fusion | flops 805306368 | bytes 9469952 | tf_op jit(solution)/shard_map/dot_general | solution.py:37
  211.7 2.7 copy.35
  214.3 4.4 %reshape.33 = f32[32,16,512]{2,1,0:T(8,128)} reshape(f32[8192,32]{1,0:T(8,128)} %copy.35) | data formatting | bytes 2097152 | tf_op jit(solution)/shard_map/reshape | solution.py:38
  218.8 3.5 %reshape_reshape.3 = f32[32,8192]{1,0:T(8,128)S(1)} reshape(f32[8192,32]{1,0:T(8,128)} %copy.35) | data formatting | bytes 2097152 | tf_op jit(solution)/shard_map/reshape;reshape | solution.py:39
  222.3 30.1 %all-gather.2.cloned.1.call-done = f32[128,16,512]{2,1,0:T(8,128)} async-done(((f32[32,16,512]{2,1,0:T(8,128)}), f32[128,16,512]{2,1,0:T(8,128)}) %all-gather.2.cloned.1.call-update) | async-done | bytes 4194320 | tf_op jit(solution)/shard_map/all_gather | solution.py:40
  252.4 5.6 %copy.40 = f32[16,8,16,512]{3,1,2,0:T(8,128)S(1)} copy(f32[16,8,16,512]{3,2,1,0:T(8,128)} %bitcast.113) | data formatting | bytes 8388608
  258.0 4.1 %fusion.38 = f32[32,128]{1,0:T(8,128)S(1)} fusion(f32[32,8192]{1,0:T(8,128)S(1)} %reshape_reshape.3, f32[128,8192]{1,0:T(8,128)S(1)} %bitcast.111), kind=kOutput, calls=%fused_computation.73 | convolution fusion | flops 402653184 | bytes 5259264 | tf_op jit(solution)/shard_map/dot_general | solution.py:42
  262.2 37.1 %psum.15 = f32[32,128]{1,0:T(8,128)S(1)} all-reduce(f32[32,128]{1,0:T(8,128)S(1)} %fusion.38), channel_id=1, replica_groups=mesh['gx'=4,'gy'=8] {'gy'}, use_global_device_ids=true, to_apply=%region_3.6 | all-reduce | flops 4096 | bytes 32768 | tf_op jit(solution)/shard_map/psum | solution.py:43
  299.2 5.5 %all_gather.7 = f32[128,128]{1,0:T(8,128)S(1)} all-gather(f32[32,128]{1,0:T(8,128)S(1)} %psum.15), channel_id=1, replica_groups=mesh['gx'=4,'gy'=8] {'gx'}, dimensions={0}, use_global_device_ids=true | all-gather | bytes 81920 | tf_op jit(solution)/shard_map/all_gather | solution.py:44
  304.8 11.7 %cholesky.45 = f32[128,128]{1,0:T(8,128)S(1)} custom-call(f32[128,128]{1,0:T(8,128)S(1)} %fusion), custom_call_target="Cholesky" | custom-call | tf_op jit(solution)/shard_map/jit(cholesky)/cholesky | solution.py:46
  317.2 0.7 multiply_bitcast_fusion
  317.9 0.7 copy.38
  (51 shorter events, 10.0 us)
Async XLA Ops:
  7.2 147.3 %copy-start = (f32[256,32]{0,1:T(8,128)S(1)}, f32[256,32]{0,1:T(8,128)}, u32[]{:S(2)}) copy-start(f32[256,32]{0,1:T(8,128)} %param.6) | copy-start | bytes 98308
  7.2 147.3 %all-reduce.2.cloned.1.call-start = ((), (), s32[]{:S(2)}) async-start(), calls=%async_computation | async-start | bytes 524288 | tf_op jit(solution)/shard_map/psum | solution.py:31
  25.0 227.4 %all-gather.2.cloned.1.call-start = ((), (), s32[]{:S(2)}) async-start(), calls=%async_computation.1 | async-start | bytes 5242880 | tf_op jit(solution)/shard_map/all_gather | solution.py:40
  201.6 17.2 %copy-start.1 = (f32[256,32]{0,1:T(8,128)}, f32[256,32]{0,1:T(8,128)S(1)}, u32[]{:S(2)}) copy-start(f32[256,32]{0,1:T(8,128)S(1)} %convolution_bitcast_fusion.2) | copy-start | bytes 98308
Sparse Core Ops, SparseCore 0:
  25.2 129.2 all-reduce.1
  218.9 33.4 all-gather.1
where the time goes:
time: 326 us; the launch traced here: 325 us
  waiting for transfers between devices  159 us (49%)
  other arithmetic  53.2 us (16%)
  blocking collectives  42.6 us (13%)
  matrix products  38.3 us (12%)
  local copies, waits for them, and re-layouts  17.4 us (5%)
  between operations  14.3 us (4%)
    psum x1, waiting for transfers between devices, local(): gram_z = lax.psum(local_gram, ('gx', 'gy'))  129 us
    psum x1, blocking collectives, local(): summed_row = lax.psum(product, 'gy')  37.1 us
    all_gather x1, waiting for transfers between devices, local(): row_piece = lax.all_gather(core_tensor, 'gx', axis=0, tiled=True)  30.1 us
    another operation x18, other arithmetic, orthonormal(): lower_factor = jnp.linalg.cholesky(inner_gram)  21.6 us
    another operation x12, other arithmetic, orthonormal(): lax.linalg.triangular_solve(lower_factor, image, left_side=False, lower=T...  18.5 us
    dot_general x1, matrix products, local(): lax.dot_general(unfolded, unfolded, (((0,), (0,)), ((), ())), precision=p...  17.8 us
    another operation x3, other arithmetic, local(): jnp.linalg.cholesky(gram_x).T / jnp.sqrt(jnp.float32(column_count))  12.4 us
    dot_general x1, matrix products, local(): jnp.dot(unfolded, z_basis, precision=precise, preferred_element_type=jnp....  10.1 us
  transfers between devices with their start and end apart: 2, of which 2 were waited for; matrix products, arithmetic and copies ran while one was open for 1% of the time, Pallas kernels for 0%

commit v1 on v0

--- a/solution.py
+++ b/solution.py
@@ -28,7 +28,7 @@
         preferred_element_type=jnp.float32,
     )
     z_basis = start_basis
-    gram_z = lax.psum(local_gram, ("gx", "gy"))
+    gram_z = lax.psum(lax.psum(local_gram, "gy"), "gx")
     for iteration in range(ITERS):
         z_basis = orthonormal(
             jnp.dot(gram_z, z_basis, precision=precise, preferred_element_type=jnp.float32)

time: 326 us -> 305 us (0.936)
  waiting for transfers between devices: 159 us -> 139 us
    psum x1 -> x2, waiting for transfers between devices: 129 us -> 107 us  [local(): gram_z = lax.psum(lax.psum(local_gram, 'gy'), 'gx')]
  transfers between devices with their start and end apart: 2 -> 3, of which waited for: 2 -> 3; matrix products, arithmetic and copies ran while one was open for 1% -> 1% of each run, Pallas kernels for 0% -> 0%
where the time goes in v1:
time: 305 us; the launch traced here: 304 us
  waiting for transfers between devices  139 us (46%)
  other arithmetic  53.2 us (17%)
  blocking collectives  42.6 us (14%)
  matrix products  38.3 us (13%)
  local copies, waits for them, and re-layouts  17.4 us (6%)
  between operations  14 us (5%)
    psum x2, waiting for transfers between devices, local(): gram_z = lax.psum(lax.psum(local_gram, 'gy'), 'gx')  107 us
    psum x1, blocking collectives, local(): summed_row = lax.psum(product, 'gy')  37.1 us
    all_gather x1, waiting for transfers between devices, local(): row_piece = lax.all_gather(core_tensor, 'gx', axis=0, tiled=True)  31.1 us
    another operation x18, other arithmetic, orthonormal(): lower_factor = jnp.linalg.cholesky(inner_gram)  21.6 us
    another operation x12, other arithmetic, orthonormal(): lax.linalg.triangular_solve(lower_factor, image, left_side=False, lower=T...  18.5 us
    dot_general x1, matrix products, local(): lax.dot_general(unfolded, unfolded, (((0,), (0,)), ((), ())), precision=p...  17.8 us
    another operation x3, other arithmetic, local(): jnp.linalg.cholesky(gram_x).T / jnp.sqrt(jnp.float32(column_count))  12.4 us
    dot_general x1, matrix products, local(): jnp.dot(unfolded, z_basis, precision=precise, preferred_element_type=jnp....  10.1 us
  transfers between devices with their start and end apart: 3, of which 3 were waited for; matrix products, arithmetic and copies ran while one was open for 1% of the time, Pallas kernels for 0%

profile of v1, /device:TPU:0, one launch (start us, length us, event | category | flops | bytes accessed | tf_op | source)
XLA Modules:
  0.0 304.3 jit_solution(13083884283183938267)
XLA Ops:
  7.2 17.8 %convolution_bitcast_fusion.1 = f32[256,256]{1,0:T(8,128)} fusion(f32[32,16,16,256]{3,2,1,0:T(8,128)} %param.5), kind=kOutput, calls=%fused_computation.1 | convolution fusion | flops 6442450944 | bytes 8650752 | tf_op jit(solution)/shard_map/dot_general | solution.py:23
  25.1 73.8 %all-reduce.3.cloned.1.call-done = f32[256,256]{1,0:T(8,128)} async-done(((f32[256,256]{1,0:T(8,128)}), f32[256,256]{1,0:T(8,128)}) %all-reduce.3.cloned.1.call-update) | async-done | bytes 262160 | tf_op jit(solution)/shard_map/psum | solution.py:31
  99.2 33.6 %all-reduce.5.cloned.1.call-done = f32[256,256]{1,0:T(8,128)} async-done(((f32[256,256]{1,0:T(8,128)}), f32[256,256]{1,0:T(8,128)}) %all-reduce.5.cloned.1.call-update) | async-done | bytes 262160 | tf_op jit(solution)/shard_map/psum | solution.py:31
  132.8 1.3 fusion.29
  134.3 2.9 cholesky.142
  137.9 0.7 fusion.1
  138.6 2.4 custom-call.13
  141.5 2.9 cholesky.153
  145.1 0.7 fusion.2
  145.8 2.4 custom-call.14
  148.4 1.3 fusion.32
  150.0 2.9 cholesky.164
  154.3 2.4 custom-call.15
  157.2 2.9 cholesky.175
  161.4 2.4 custom-call.16
  164.1 1.3 fusion.35
  165.7 2.9 cholesky.186
  169.9 2.4 custom-call.17
  172.9 2.9 cholesky.197
  177.1 2.4 custom-call.18
  179.8 10.1 %convolution_bitcast_fusion = f32[8192,32]{0,1:T(8,128)S(1)} fusion(f32[256,32]{0,1:T(8,128)S(1)} %convolution_bitcast_fusion.2, f32[8192,256]{1,0:T(8,128)} %bitcast.112), kind=kOutput, calls=%fused_computation | convolution fusion | flops 805306368 | bytes 9469952 | tf_op jit(solution)/shard_map/dot_general | solution.py:37
  189.9 2.7 copy.35
  192.6 4.4 %reshape.33 = f32[32,16,512]{2,1,0:T(8,128)} reshape(f32[8192,32]{1,0:T(8,128)} %copy.35) | data formatting | bytes 2097152 | tf_op jit(solution)/shard_map/reshape | solution.py:38
  197.0 3.5 %reshape_reshape.3 = f32[32,8192]{1,0:T(8,128)S(1)} reshape(f32[8192,32]{1,0:T(8,128)} %copy.35) | data formatting | bytes 2097152 | tf_op jit(solution)/shard_map/reshape;reshape | solution.py:39
  200.5 31.1 %all-gather.2.cloned.1.call-done = f32[128,16,512]{2,1,0:T(8,128)} async-done(((f32[32,16,512]{2,1,0:T(8,128)}), f32[128,16,512]{2,1,0:T(8,128)}) %all-gather.2.cloned.1.call-update) | async-done | bytes 4194320 | tf_op jit(solution)/shard_map/all_gather | solution.py:40
  231.6 5.6 %copy.40 = f32[16,8,16,512]{3,1,2,0:T(8,128)S(1)} copy(f32[16,8,16,512]{3,2,1,0:T(8,128)} %bitcast.113) | data formatting | bytes 8388608
  237.2 4.1 %fusion.38 = f32[32,128]{1,0:T(8,128)S(1)} fusion(f32[32,8192]{1,0:T(8,128)S(1)} %reshape_reshape.3, f32[128,8192]{1,0:T(8,128)S(1)} %bitcast.111), kind=kOutput, calls=%fused_computation.73 | convolution fusion | flops 402653184 | bytes 5259264 | tf_op jit(solution)/shard_map/dot_general | solution.py:42
  241.4 37.1 %psum.23 = f32[32,128]{1,0:T(8,128)S(1)} all-reduce(f32[32,128]{1,0:T(8,128)S(1)} %fusion.38), channel_id=1, replica_groups=mesh['gx'=4,'gy'=8] {'gy'}, use_global_device_ids=true, to_apply=%region_4.7 | all-reduce | flops 4096 | bytes 32768 | tf_op jit(solution)/shard_map/psum | solution.py:43
  278.4 5.5 %all_gather.7 = f32[128,128]{1,0:T(8,128)S(1)} all-gather(f32[32,128]{1,0:T(8,128)S(1)} %psum.23), channel_id=1, replica_groups=mesh['gx'=4,'gy'=8] {'gx'}, dimensions={0}, use_global_device_ids=true | all-gather | bytes 81920 | tf_op jit(solution)/shard_map/all_gather | solution.py:44
  284.0 11.7 %cholesky.45 = f32[128,128]{1,0:T(8,128)S(1)} custom-call(f32[128,128]{1,0:T(8,128)S(1)} %fusion), custom_call_target="Cholesky" | custom-call | tf_op jit(solution)/shard_map/jit(cholesky)/cholesky | solution.py:46
  296.4 0.7 multiply_bitcast_fusion
  297.1 0.7 copy.38
  (54 shorter events, 10.7 us)
Async XLA Ops:
  7.2 125.6 %copy-start = (f32[256,32]{0,1:T(8,128)S(1)}, f32[256,32]{0,1:T(8,128)}, u32[]{:S(2)}) copy-start(f32[256,32]{0,1:T(8,128)} %param.6) | copy-start | bytes 98308
  7.2 91.7 %all-reduce.3.cloned.1.call-start = ((), (), s32[]{:S(2)}) async-start(), calls=%async_computation | async-start | bytes 524288 | tf_op jit(solution)/shard_map/psum | solution.py:31
  25.0 107.7 %all-reduce.5.cloned.1.call-start = ((), (), s32[]{:S(2)}) async-start(), calls=%async_computation.1 | async-start | bytes 524288 | tf_op jit(solution)/shard_map/psum | solution.py:31
  98.9 132.7 %all-gather.2.cloned.1.call-start = ((), (), s32[]{:S(2)}) async-start(), calls=%async_computation.2 | async-start | bytes 5242880 | tf_op jit(solution)/shard_map/all_gather | solution.py:40
  179.8 17.2 %copy-start.1 = (f32[256,32]{0,1:T(8,128)}, f32[256,32]{0,1:T(8,128)S(1)}, u32[]{:S(2)}) copy-start(f32[256,32]{0,1:T(8,128)S(1)} %convolution_bitcast_fusion.2) | copy-start | bytes 98308
Sparse Core Ops, SparseCore 0:
  25.2 73.7 all-reduce.2
  101.2 31.4 all-reduce.4
  197.1 34.4 all-gather.1

commit v2 on v0

--- a/solution.py
+++ b/solution.py
@@ -37,7 +37,9 @@
     core_rows = jnp.dot(unfolded, z_basis, precision=precise, preferred_element_type=jnp.float32)
     core_tensor = core_rows.reshape(x_cells, y_cells, species * rank_kept)
     own_rows = core_tensor.reshape(x_cells, -1)
-    row_piece = lax.all_gather(core_tensor, "gx", axis=0, tiled=True)
+    row_piece = jnp.concatenate(
+        lax.all_to_all(jnp.stack([core_tensor] * lax.axis_size("gx")), "gx", 0, 0), axis=0
+    )
     piece_rows = row_piece.reshape(row_piece.shape[0], -1)
     product = jnp.dot(own_rows, piece_rows.T, precision=precise, preferred_element_type=jnp.float32)
     summed_row = lax.psum(product, "gy")

time: 326 us -> 346 us (1.061)
  waiting for transfers between devices: 159 us -> 174 us
  starting transfers between devices: 0.26 us -> 4.9 us
    all_to_all x0 -> x1, waiting for transfers between devices: none -> 44.7 us  [local(): lax.all_to_all(jnp.stack([core_tensor] * lax.axis_size('gx')), 'gx', 0, 0)]
    all_gather x1 -> x0, waiting for transfers between devices: 30.1 us -> none  [local(): row_piece = lax.all_gather(core_tensor, 'gx', axis=0, tiled=True)]
    all_to_all x0 -> x1, starting transfers between devices: none -> 4.86 us  [local(): lax.all_to_all(jnp.stack([core_tensor] * lax.axis_size('gx')), 'gx', 0, 0)]
where the time goes in v2:
time: 346 us; the launch traced here: 345 us
  waiting for transfers between devices  174 us (50%)
  other arithmetic  53.2 us (15%)
  blocking collectives  41.3 us (12%)
  matrix products  38.2 us (11%)
  local copies, waits for them, and re-layouts  19.1 us (6%)
  between operations  14.3 us (4%)
  starting transfers between devices  4.9 us (1%)
    psum x1, waiting for transfers between devices, local(): gram_z = lax.psum(local_gram, ('gx', 'gy'))  129 us
    all_to_all x1, waiting for transfers between devices, local(): lax.all_to_all(jnp.stack([core_tensor] * lax.axis_size('gx')), 'gx', 0, 0)  44.7 us
    psum x1, blocking collectives, local(): summed_row = lax.psum(product, 'gy')  36.1 us
    another operation x18, other arithmetic, orthonormal(): lower_factor = jnp.linalg.cholesky(inner_gram)  21.6 us
    another operation x12, other arithmetic, orthonormal(): lax.linalg.triangular_solve(lower_factor, image, left_side=False, lower=T...  18.5 us
    dot_general x1, matrix products, local(): lax.dot_general(unfolded, unfolded, (((0,), (0,)), ((), ())), precision=p...  17.7 us
    another operation x3, other arithmetic, local(): jnp.linalg.cholesky(gram_x).T / jnp.sqrt(jnp.float32(column_count))  12.4 us
    dot_general x1, matrix products, local(): jnp.dot(unfolded, z_basis, precision=precise, preferred_element_type=jnp....  10 us
  transfers between devices with their start and end apart: 2, of which 2 were waited for; matrix products, arithmetic and copies ran while one was open for 1% of the time, Pallas kernels for 0%

profile of v2, /device:TPU:0, one launch (start us, length us, event | category | flops | bytes accessed | tf_op | source)
XLA Modules:
  0.0 345.2 jit_solution(9829408684265592677)
XLA Ops:
  7.2 17.7 %convolution_bitcast_fusion.1 = f32[256,256]{1,0:T(8,128)} fusion(f32[32,16,16,256]{3,2,1,0:T(8,128)} %param.5), kind=kOutput, calls=%fused_computation.1 | convolution fusion | flops 6442450944 | bytes 8650752 | tf_op jit(solution)/shard_map/dot_general | solution.py:23
  24.9 129.5 %all-reduce.2.cloned.1.call-done = f32[256,256]{1,0:T(8,128)} async-done(((f32[256,256]{1,0:T(8,128)}), f32[256,256]{1,0:T(8,128)}) %all-reduce.2.cloned.1.call-update) | async-done | bytes 262160 | tf_op jit(solution)/shard_map/psum | solution.py:31
  154.4 1.3 fusion.29
  156.0 2.9 cholesky.142
  159.6 0.7 fusion.1
  160.2 2.4 custom-call.13
  163.2 2.9 cholesky.153
  167.4 2.4 custom-call.14
  170.1 1.3 fusion.32
  171.7 2.9 cholesky.164
  175.9 2.4 custom-call.15
  178.9 2.9 cholesky.175
  183.1 2.4 custom-call.16
  185.8 1.3 fusion.35
  187.4 2.9 cholesky.186
  191.6 2.4 custom-call.17
  194.6 2.9 cholesky.197
  198.8 2.4 custom-call.18
  201.5 10.0 %convolution_bitcast_fusion = f32[8192,32]{0,1:T(8,128)S(1)} fusion(f32[256,32]{0,1:T(8,128)S(1)} %convolution_bitcast_fusion.2, f32[8192,256]{1,0:T(8,128)} %bitcast.113), kind=kOutput, calls=%fused_computation | convolution fusion | flops 805306368 | bytes 9469952 | tf_op jit(solution)/shard_map/dot_general | solution.py:37
  211.6 2.7 copy.35
  214.2 3.5 %reshape.32 = f32[32,16,512]{2,1,0:T(8,128)S(1)} reshape(f32[8192,32]{1,0:T(8,128)} %copy.35) | data formatting | bytes 2097152 | tf_op jit(solution)/shard_map/reshape | solution.py:38
  217.8 2.5 stack.3
  220.3 4.9 %all-to-all-start = ((f32[4,32,16,512]{3,2,1,0:T(8,128)}), f32[4,32,16,512]{3,2,1,0:T(8,128)}, u32[]{:S(2)}, u32[]{:S(2)}) async-start(f32[4,32,16,512]{3,2,1,0:T(8,128)} %stack.3), calls=%async_computation | async-start | bytes 8388608 | tf_op jit(solution)/shard_map/all_to_all | solution.py:41
  225.2 3.5 %reshape_reshape.6 = f32[32,8192]{1,0:T(8,128)S(1)} reshape(f32[8192,32]{1,0:T(8,128)} %copy.35) | data formatting | bytes 2097152 | tf_op jit(solution)/shard_map/reshape;reshape | solution.py:39
  228.7 44.7 %all-to-all-done = f32[4,32,16,512]{3,2,1,0:T(8,128)} async-done(((f32[4,32,16,512]{3,2,1,0:T(8,128)}), f32[4,32,16,512]{3,2,1,0:T(8,128)}, u32[]{:S(2)}, u32[]{:S(2)}) %all-to-all-start) | async-done | bytes 4194336 | tf_op jit(solution)/shard_map/all_to_all | solution.py:41
  273.4 5.6 %copy.40 = f32[16,8,16,512]{3,1,2,0:T(8,128)S(1)} copy(f32[16,8,16,512]{3,2,1,0:T(8,128)} %bitcast.32) | data formatting | bytes 8388608
  279.0 4.1 %fusion.38 = f32[32,128]{1,0:T(8,128)S(1)} fusion(f32[32,8192]{1,0:T(8,128)S(1)} %reshape_reshape.6, f32[128,8192]{1,0:T(8,128)S(1)} %bitcast.112), kind=kOutput, calls=%fused_computation.73 | convolution fusion | flops 402653184 | bytes 5259264 | tf_op jit(solution)/shard_map/dot_general | solution.py:44
  283.1 36.1 %psum.15 = f32[32,128]{1,0:T(8,128)S(1)} all-reduce(f32[32,128]{1,0:T(8,128)S(1)} %fusion.38), channel_id=1, replica_groups=mesh['gx'=4,'gy'=8] {'gy'}, use_global_device_ids=true, to_apply=%region_3.6 | all-reduce | flops 4096 | bytes 32768 | tf_op jit(solution)/shard_map/psum | solution.py:45
  319.3 5.2 %all_gather.3 = f32[128,128]{1,0:T(8,128)S(1)} all-gather(f32[32,128]{1,0:T(8,128)S(1)} %psum.15), channel_id=1, replica_groups=mesh['gx'=4,'gy'=8] {'gx'}, dimensions={0}, use_global_device_ids=true | all-gather | bytes 81920 | tf_op jit(solution)/shard_map/all_gather | solution.py:46
  324.6 11.7 %cholesky.45 = f32[128,128]{1,0:T(8,128)S(1)} custom-call(f32[128,128]{1,0:T(8,128)S(1)} %fusion), custom_call_target="Cholesky" | custom-call | tf_op jit(solution)/shard_map/jit(cholesky)/cholesky | solution.py:48
  337.0 0.7 multiply_bitcast_fusion
  337.6 0.7 copy.38
  (53 shorter events, 11.1 us)
Async XLA Ops:
  7.2 147.3 %copy-start = (f32[256,32]{0,1:T(8,128)S(1)}, f32[256,32]{0,1:T(8,128)}, u32[]{:S(2)}) copy-start(f32[256,32]{0,1:T(8,128)} %param.6) | copy-start | bytes 98308
  7.2 147.3 %all-reduce.2.cloned.1.call-start = ((), (), s32[]{:S(2)}) async-start(), calls=%async_computation.1 | async-start | bytes 524288 | tf_op jit(solution)/shard_map/psum | solution.py:31
  201.5 16.3 %copy-start.2 = (f32[256,32]{0,1:T(8,128)}, f32[256,32]{0,1:T(8,128)S(1)}, u32[]{:S(2)}) copy-start(f32[256,32]{0,1:T(8,128)S(1)} %convolution_bitcast_fusion.2) | copy-start | bytes 98308
  217.8 10.9 %copy-start.1 = (f32[32,16,512]{2,1,0:T(8,128)}, f32[32,16,512]{2,1,0:T(8,128)S(1)}, u32[]{:S(2)}) copy-start(f32[32,16,512]{2,1,0:T(8,128)S(1)} %reshape.32) | copy-start | bytes 3145732
  220.3 53.1 %all-to-all-start = ((f32[4,32,16,512]{3,2,1,0:T(8,128)}), f32[4,32,16,512]{3,2,1,0:T(8,128)}, u32[]{:S(2)}, u32[]{:S(2)}) async-start(f32[4,32,16,512]{3,2,1,0:T(8,128)} %stack.3), calls=%async_computation | async-start | bytes 8388608 | tf_op jit(solution)/shard_map/all_to_all | solution.py:41
Sparse Core Ops, SparseCore 0:
  25.1 129.3 all-reduce.1
